TPU v7x, 256 devices: a whole 4x4x8 slice. The times are simulated.
256 devices in a mesh: pipe: 16 (over z_hi, y, core), dp: 16 (over x, z_lo).
Axes of the slice: x: 4, y: 4, z: 8 (z_hi: 2, z_lo: 4; z = z_hi * 4 + z_lo), core: 2. Of those that a mesh axis runs over, the one named last changes fastest.
Arguments:
- weights: bfloat16 [16, 2, 7168, 256], P('pipe'), may hold values from -0.375 to 0.375
- gain_model: bfloat16 [16, 7168], P('pipe'), may hold values from 0.099609375 to 1.8984375
- gain_latent: bfloat16 [16, 256], P('pipe'), may hold values from 0.099609375 to 1.8984375
- saved_down: bfloat16 [16, 2, 512, 7168], P('pipe', None, 'dp'), may hold values from -6 to 6
- saved_up: bfloat16 [16, 2, 512, 7168], P('pipe', None, 'dp'), may hold values from -6 to 6
- grad_start: bfloat16 [2, 16, 512, 7168], P(None, 'pipe', 'dp'), may hold values from -0.119628906 to 0.119628906
Outputs:
- section_grads: bfloat16 [16, 2, 7168, 256], P('pipe', None, 'dp')
All inputs are finite; a program needn't handle non-finite values.
Results may differ from a plain program's by a relative error of at most 0.024.
Values may be sent and summed in bfloat16 or wider, within the bound.
A program may use at most 128 MiB of HBM per device.

v0:
```python
import jax
import jax.numpy as jnp
from jax import lax
from jax.sharding import PartitionSpec as P

EPS = 1e-06


def from_partner(block, axis, apart):
    count = lax.axis_size(axis)
    route = []
    for low in range(count):
        high = low | 1 << apart
        if high != low and high < count:
            route += [(low, high), (high, low)]
    return lax.ppermute(block, axis, route)


def from_behind(block, axis, distance):
    devices = range(lax.axis_size(axis))
    route = [(i - distance, i) for i in devices if i - distance in devices]
    return lax.ppermute(block, axis, route)


def contract(left, right):
    return lax.dot_general(
        left, right, (((0,), (0,)), ((), ())), preferred_element_type=jnp.float32
    )


def micro(inputs, incoming, pair, gain_in, gain_lat, need_input):
    xf = inputs.astype(jnp.float32)
    inv_in = lax.rsqrt(jnp.mean(xf * xf, axis=-1, keepdims=True) + EPS)
    normed = (xf * inv_in * gain_in.astype(jnp.float32)).astype(jnp.bfloat16)
    latent = jnp.dot(normed, pair[0], preferred_element_type=jnp.float32)
    inv_lat = lax.rsqrt(jnp.mean(latent * latent, axis=-1, keepdims=True) + EPS)
    keyed = (latent * inv_lat * gain_lat.astype(jnp.float32)).astype(jnp.bfloat16)
    dkey = jnp.dot(incoming, pair[1], preferred_element_type=jnp.float32)
    scaled = dkey * gain_lat.astype(jnp.float32)
    dlat = (
        inv_lat
        * (scaled - latent * inv_lat * inv_lat * jnp.mean(scaled * latent, axis=-1, keepdims=True))
    ).astype(jnp.bfloat16)
    terms = jnp.stack([contract(normed, dlat), contract(incoming, keyed)])
    result = None
    if need_input:
        dnorm = lax.dot_general(
            dlat, pair[0], (((1,), (1,)), ((), ())), preferred_element_type=jnp.float32
        )
        vgrad = dnorm * gain_in.astype(jnp.float32)
        result = (
            incoming.astype(jnp.float32)
            + inv_in * (vgrad - xf * inv_in * inv_in * jnp.mean(vgrad * xf, axis=-1, keepdims=True))
        ).astype(jnp.bfloat16)
    return (result, terms)


def per_device(weights, gain_model, gain_latent, saved_down, saved_up, grad_start):
    bits = lax.axis_size("pipe").bit_length() - 1
    replicas = lax.axis_size("dp")
    replica = lax.axis_index("dp")
    own = weights[0]
    own_in = gain_model[0]
    own_lat = gain_latent[0]
    share = own.shape[1] // replicas
    carried = (lax.dynamic_slice_in_dim(own, replica * share, share, 1), own_in, own_lat)
    for bit in range(bits):
        carried = from_partner((carried[0], carried[1], carried[2]), "pipe", bit)
    other_piece, other_in, other_lat = carried
    other = lax.all_gather(other_piece, "dp", axis=1, tiled=True)
    down_grad, down_first = micro(saved_down[0, 0], grad_start[0, 0], own, own_in, own_lat, True)
    up_grad, up_first = micro(saved_up[0, 0], grad_start[1, 0], other, other_in, other_lat, True)
    from_above = from_behind(down_grad, "pipe", -1)
    from_below = from_behind(up_grad, "pipe", 1)
    unused_down, down_second = micro(saved_down[0, 1], from_above, own, own_in, own_lat, False)
    unused_up, up_second = micro(saved_up[0, 1], from_below, other, other_in, other_lat, False)
    own_part, other_part = (
        lax.psum_scatter(
            (down_first + down_second).astype(jnp.bfloat16), "dp", scatter_dimension=1, tiled=True
        ).astype(jnp.float32),
        lax.psum_scatter(
            (up_first + up_second).astype(jnp.bfloat16), "dp", scatter_dimension=1, tiled=True
        ).astype(jnp.float32),
    )
    returned = other_part
    for bit in range(bits):
        returned = from_partner(returned.astype(jnp.bfloat16), "pipe", bit).astype(returned.dtype)
    total = own_part + returned
    return total.astype(jnp.bfloat16)[None]


def solution(mesh):
    placed = (
        P("pipe", None, None, None),
        P("pipe", None),
        P("pipe", None),
        P("pipe", None, "dp", None),
        P("pipe", None, "dp", None),
        P(None, "pipe", "dp", None),
    )
    return jax.shard_map(
        per_device,
        mesh=mesh,
        in_specs=placed,
        out_specs=P("pipe", None, "dp", None),
        check_vma=False,
    )
```

profile of v0, /device:TPU:24, one launch (start us, length us, event | category | flops | bytes accessed | tf_op | source)
XLA Modules:
  0.0 618.5 jit_solution(15179174471930431050)
XLA Ops:
  6.5 1.1 dynamic-slice_bitcast_fusion
  7.7 0.1 collective-permute-start.5
  7.8 1.8 collective-permute-done.5
  9.6 0.7 collective-permute-start.6
  10.3 11.8 %collective-permute-done.6 = bf16[2,448,256]{2,1,0:T(8,128)(2,1)S(1)} collective-permute-done((bf16[2,448,256]{2,1,0:T(8,128)(2,1)S(1)}, bf16[2,448,256]{2,1,0:T(8,128)(2,1)S(1)}, u32[]{:S(2)}, u32[]{:S(2)}) %collective-permute-start.6) | collective-permute-done | bytes 458784 | tf_op jit(solution)/shard_map/ppermute | solution.py:16
  22.1 1.7 collective-permute-start.7
  23.8 11.6 %collective-permute-done.7 = bf16[2,448,256]{2,1,0:T(8,128)(2,1)S(1)} collective-permute-done((bf16[2,448,256]{2,1,0:T(8,128)(2,1)S(1)}, bf16[2,448,256]{2,1,0:T(8,128)(2,1)S(1)}, u32[]{:S(2)}, u32[]{:S(2)}) %collective-permute-start.7) | collective-permute-done | bytes 458784 | tf_op jit(solution)/shard_map/ppermute | solution.py:16
  35.4 7.2 %collective-permute-start.8 = (bf16[2,448,256]{2,1,0:T(8,128)(2,1)S(1)}, bf16[2,448,256]{2,1,0:T(8,128)(2,1)S(1)}, u32[]{:S(2)}, u32[]{:S(2)}) collective-permute-start(bf16[2,448,256]{2,1,0:T(8,128)(2,1)S(1)} %collective-permute-done.7), channel_id=1, source_target_pairs={{0,128},{128,0},{16,144},{144,16},{32,160},{160,32},{48,176},{176,... | collective-permute-start | bytes 1376264 | tf_op jit(solution)/shard_map/ppermute | solution.py:16
  42.6 11.3 %collective-permute-done.8 = bf16[2,448,256]{2,1,0:T(8,128)(2,1)S(1)} collective-permute-done((bf16[2,448,256]{2,1,0:T(8,128)(2,1)S(1)}, bf16[2,448,256]{2,1,0:T(8,128)(2,1)S(1)}, u32[]{:S(2)}, u32[]{:S(2)}) %collective-permute-start.8) | collective-permute-done | bytes 458784 | tf_op jit(solution)/shard_map/ppermute | solution.py:16
  53.9 0.8 copy-done.4
  54.7 0.0 reduce-scatter.5.cloned.1.call-start
  54.7 0.8 reduce
  55.6 0.1 collective-permute-start.1
  55.7 0.7 reduce.1
  56.4 0.6 collective-permute-start.9
  57.0 1.5 fusion.55
  58.4 3.1 fusion.9
  61.6 3.1 multiply_reduce_fusion.6
  64.7 0.1 multiply_convert_fusion.7
  64.8 2.2 fusion.59
  67.0 0.8 collective-permute-start.10
  67.9 1.3 collective-permute-start.2
  69.2 0.2 fusion.64
  69.4 1.3 collective-permute-done.10
  70.7 1.2 collective-permute-start.11
  71.9 2.3 collective-permute-start.3
  74.2 1.5 collective-permute-done.11
  75.7 12.6 %collective-permute-start.12 = (bf16[256]{0:T(256)(128)(2,1)S(1)}, bf16[256]{0:T(256)(128)(2,1)S(1)}, u32[]{:S(2)}, u32[]{:S(2)}) collective-permute-start(bf16[256]{0:T(256)(128)(2,1)S(1)} %collective-permute-done.11), channel_id=1, source_target_pairs={{0,128},{128,0},{16,144},{144,16},{32,160},{160,32},{48,176},{176,... | collective-permute-start | bytes 1544 | tf_op jit(solution)/shard_map/ppermute | solution.py:16
  88.3 1.4 collective-permute-start.4
  89.8 0.3 collective-permute-done.12
  90.0 6.2 %collective-permute-done.4 = bf16[7168]{0:T(1024)(128)(2,1)S(1)} collective-permute-done((bf16[7168]{0:T(1024)(128)(2,1)S(1)}, bf16[7168]{0:T(1024)(128)(2,1)S(1)}, u32[]{:S(2)}, u32[]{:S(2)}) %collective-permute-start.4) | collective-permute-done | bytes 14368 | tf_op jit(solution)/shard_map/ppermute | solution.py:16
  96.3 132.2 %all-gather.2.cloned.1.call-done = bf16[2,7168,256]{2,1,0:T(8,128)(2,1)} async-done(((bf16[2,448,256]{2,1,0:T(8,128)(2,1)}), bf16[2,7168,256]{2,1,0:T(8,128)(2,1)}) %all-gather.2.cloned.1.call-update) | async-done | bytes 7340048 | tf_op jit(solution)/shard_map/all_gather | solution.py:70
  228.4 3.0 fusion.16
  231.5 3.0 multiply_reduce_fusion.2
  234.5 0.1 multiply_convert_fusion.3
  234.6 1.3 convolution_bitcast_fusion.3
  235.9 1.3 fusion.68
  237.2 0.6 fusion.54
  237.8 1.9 collective-permute-start.13
  239.8 1.2 convolution_bitcast_fusion.2
  240.9 0.8 fusion.15
  241.7 5.9 collective-permute-done.13
  247.6 0.8 multiply_reduce_fusion
  248.5 1.3 convolution_bitcast_fusion.1
  249.8 1.2 convolution_bitcast_fusion
  250.9 4.0 fusion.1
  255.0 1.3 convolution_bitcast_fusion.7
  256.3 2.4 collective-permute-start
  258.7 1.2 convolution_bitcast_fusion.6
  259.9 2.8 fusion.7
  262.7 1.8 collective-permute-done
  264.5 0.8 multiply_reduce_fusion.4
  265.3 1.2 convolution_bitcast_fusion.4
  266.5 1.3 convolution_bitcast_fusion.5
  267.8 4.0 fusion
  271.8 153.0 %reduce-scatter.5.cloned.1.call-done = bf16[2,448,256]{2,1,0:T(8,128)(2,1)} async-done(((bf16[2,7168,256]{2,1,0:T(8,128)(2,1)}), bf16[2,448,256]{2,1,0:T(8,128)(2,1)}) %reduce-scatter.5.cloned.1.call-update) | async-done | bytes 458768 | tf_op jit(solution)/shard_map/reduce_scatter | solution.py:81
  424.8 2.0 collective-permute-done.14
  426.8 0.8 collective-permute-start.15
  427.7 11.7 %collective-permute-done.15 = bf16[2,448,256]{2,1,0:T(8,128)(2,1)S(1)} collective-permute-done((bf16[2,448,256]{2,1,0:T(8,128)(2,1)S(1)}, bf16[2,448,256]{2,1,0:T(8,128)(2,1)S(1)}, u32[]{:S(2)}, u32[]{:S(2)}) %collective-permute-start.15) | collective-permute-done | bytes 458784 | tf_op jit(solution)/shard_map/ppermute | solution.py:16
  439.4 5.0 collective-permute-start.16
  444.3 10.4 %collective-permute-done.16 = bf16[2,448,256]{2,1,0:T(8,128)(2,1)S(1)} collective-permute-done((bf16[2,448,256]{2,1,0:T(8,128)(2,1)S(1)}, bf16[2,448,256]{2,1,0:T(8,128)(2,1)S(1)}, u32[]{:S(2)}, u32[]{:S(2)}) %collective-permute-start.16) | collective-permute-done | bytes 458784 | tf_op jit(solution)/shard_map/ppermute | solution.py:16
  454.8 0.9 collective-permute-start.17
  455.7 154.4 %reduce-scatter.3.cloned.1.call-done = bf16[2,448,256]{2,1,0:T(8,128)(2,1)} async-done(((bf16[2,7168,256]{2,1,0:T(8,128)(2,1)}), bf16[2,448,256]{2,1,0:T(8,128)(2,1)}) %reduce-scatter.3.cloned.1.call-update) | async-done | bytes 458768 | tf_op jit(solution)/shard_map/reduce_scatter | solution.py:78
  610.1 1.9 fusion.73
  (48 shorter events, 0.2 us)
Async XLA Ops:
  6.5 58.2 %copy-start.1 = (bf16[1,2,32,7168]{3,2,1,0:T(8,128)(2,1)S(1)}, bf16[1,2,32,7168]{3,2,1,0:T(8,128)(2,1)}, u32[]{:S(2)}) copy-start(bf16[1,2,32,7168]{3,2,1,0:T(8,128)(2,1)} %param.9) | copy-start | bytes 2752516
  6.5 221.9 %all-gather.2.cloned.1.call-start = ((), (), s32[]{:S(2)}) async-start(), calls=%async_computation.3 | async-start | bytes 7798784 | tf_op jit(solution)/shard_map/all_gather | solution.py:70
  7.7 1.9 collective-permute-start.5
  9.6 12.6 %collective-permute-start.6 = (bf16[2,448,256]{2,1,0:T(8,128)(2,1)S(1)}, bf16[2,448,256]{2,1,0:T(8,128)(2,1)S(1)}, u32[]{:S(2)}, u32[]{:S(2)}) collective-permute-start(bf16[2,448,256]{2,1,0:T(8,128)(2,1)S(1)} %collective-permute-done.5), channel_id=1, source_target_pairs={{0,32},{32,0},{16,48},{48,16},{64,96},{96,64},{80,112},{112,80},{1... | collective-permute-start | bytes 1376264 | tf_op jit(solution)/shard_map/ppermute | solution.py:16
  22.1 13.2 %collective-permute-start.7 = (bf16[2,448,256]{2,1,0:T(8,128)(2,1)S(1)}, bf16[2,448,256]{2,1,0:T(8,128)(2,1)S(1)}, u32[]{:S(2)}, u32[]{:S(2)}) collective-permute-start(bf16[2,448,256]{2,1,0:T(8,128)(2,1)S(1)} %collective-permute-done.6), channel_id=1, source_target_pairs={{0,64},{64,0},{16,80},{80,16},{32,96},{96,32},{48,112},{112,48},{1... | collective-permute-start | bytes 1376264 | tf_op jit(solution)/shard_map/ppermute | solution.py:16
  35.4 18.5 %collective-permute-start.8 = (bf16[2,448,256]{2,1,0:T(8,128)(2,1)S(1)}, bf16[2,448,256]{2,1,0:T(8,128)(2,1)S(1)}, u32[]{:S(2)}, u32[]{:S(2)}) collective-permute-start(bf16[2,448,256]{2,1,0:T(8,128)(2,1)S(1)} %collective-permute-done.7), channel_id=1, source_target_pairs={{0,128},{128,0},{16,144},{144,16},{32,160},{160,32},{48,176},{176,... | collective-permute-start | bytes 1376264 | tf_op jit(solution)/shard_map/ppermute | solution.py:16
  53.9 0.8 copy-start.4
  54.7 370.1 %reduce-scatter.5.cloned.1.call-start = ((), (), s32[]{:S(2)}) async-start(), calls=%async_computation.4 | async-start | bytes 7798784 | tf_op jit(solution)/shard_map/reduce_scatter | solution.py:81
  55.6 12.3 %collective-permute-start.1 = (bf16[7168]{0:T(1024)(128)(2,1)S(1)}, bf16[7168]{0:T(1024)(128)(2,1)S(1)}, u32[]{:S(2)}, u32[]{:S(2)}) collective-permute-start(bf16[7168]{0:T(1024)(128)(2,1)S(1)} %reduce), channel_id=1, source_target_pairs={{0,16},{16,0},{32,48},{48,32},{64,80},{80,64},{96,112},{112,96},{1... | collective-permute-start | bytes 43016 | tf_op jit(solution)/shard_map/ppermute | solution.py:16
  56.4 8.4 %copy-start.5 = (bf16[1,2,7168,256]{3,2,1,0:T(8,128)(2,1)S(1)}, bf16[1,2,7168,256]{3,2,1,0:T(8,128)(2,1)}, u32[]{:S(2)}) copy-start(bf16[1,2,7168,256]{3,2,1,0:T(8,128)(2,1)} %param.6) | copy-start | bytes 22020100
  56.4 10.7 %collective-permute-start.9 = (bf16[256]{0:T(256)(128)(2,1)S(1)}, bf16[256]{0:T(256)(128)(2,1)S(1)}, u32[]{:S(2)}, u32[]{:S(2)}) collective-permute-start(bf16[256]{0:T(256)(128)(2,1)S(1)} %reduce.1), channel_id=1, source_target_pairs={{0,16},{16,0},{32,48},{48,32},{64,80},{80,64},{96,112},{112,96},{1... | collective-permute-start | bytes 1544 | tf_op jit(solution)/shard_map/ppermute | solution.py:16
  58.4 10.7 %copy-start = (bf16[1,2,32,7168]{3,2,1,0:T(8,128)(2,1)S(1)}, bf16[1,2,32,7168]{3,2,1,0:T(8,128)(2,1)}, u32[]{:S(2)}) copy-start(bf16[1,2,32,7168]{3,2,1,0:T(8,128)(2,1)} %param.10) | copy-start | bytes 2752516
  61.6 169.9 %copy-start.2 = (bf16[2,1,32,7168]{3,2,1,0:T(8,128)(2,1)S(1)}, bf16[2,1,32,7168]{3,2,1,0:T(8,128)(2,1)}, u32[]{:S(2)}) copy-start(bf16[2,1,32,7168]{3,2,1,0:T(8,128)(2,1)} %param.11) | copy-start | bytes 2752516
  67.0 3.6 collective-permute-start.10
  67.9 4.0 collective-permute-start.2
  70.7 5.0 collective-permute-start.11
  71.9 16.4 %collective-permute-start.3 = (bf16[7168]{0:T(1024)(128)(2,1)S(1)}, bf16[7168]{0:T(1024)(128)(2,1)S(1)}, u32[]{:S(2)}, u32[]{:S(2)}) collective-permute-start(bf16[7168]{0:T(1024)(128)(2,1)S(1)} %collective-permute-done.2), channel_id=1, source_target_pairs={{0,64},{64,0},{16,80},{80,16},{32,96},{96,32},{48,112},{112,48},{1... | collective-permute-start | bytes 43016 | tf_op jit(solution)/shard_map/ppermute | solution.py:16
  75.7 14.3 %collective-permute-start.12 = (bf16[256]{0:T(256)(128)(2,1)S(1)}, bf16[256]{0:T(256)(128)(2,1)S(1)}, u32[]{:S(2)}, u32[]{:S(2)}) collective-permute-start(bf16[256]{0:T(256)(128)(2,1)S(1)} %collective-permute-done.11), channel_id=1, source_target_pairs={{0,128},{128,0},{16,144},{144,16},{32,160},{160,32},{48,176},{176,... | collective-permute-start | bytes 1544 | tf_op jit(solution)/shard_map/ppermute | solution.py:16
  88.3 7.9 %collective-permute-start.4 = (bf16[7168]{0:T(1024)(128)(2,1)S(1)}, bf16[7168]{0:T(1024)(128)(2,1)S(1)}, u32[]{:S(2)}, u32[]{:S(2)}) collective-permute-start(bf16[7168]{0:T(1024)(128)(2,1)S(1)} %collective-permute-done.3), channel_id=1, source_target_pairs={{0,128},{128,0},{16,144},{144,16},{32,160},{160,32},{48,176},{176,... | collective-permute-start | bytes 43016 | tf_op jit(solution)/shard_map/ppermute | solution.py:16
  228.4 7.4 %slice-start.2 = ((s8[7340032]{0:T(1024)(128)(4,1)}), s8[4194304]{0:T(1024)(128)(4,1)S(1)}, s32[]{:S(2)}) async-start(s8[7340032]{0:T(1024)(128)(4,1)} %bitcast.191), calls=%async_computation.7 | async-start | bytes 8388608
  231.4 4.4 slice-start.3
  234.5 2.7 copy-start.3
  237.8 9.8 %collective-permute-start.13 = (bf16[32,7168]{1,0:T(8,128)(2,1)S(1)}, bf16[32,7168]{1,0:T(8,128)(2,1)S(1)}, u32[]{:S(2)}, u32[]{:S(2)}) collective-permute-start(bf16[32,7168]{1,0:T(8,128)(2,1)S(1)} %get-tuple-element.18), channel_id=1, source_target_pairs={{0,16},{16,32},{32,48},{48,64},{64,80},{80,96},{96,112},{112,128},... | collective-permute-start | bytes 1376264 | tf_op jit(solution)/shard_map/ppermute | solution.py:22
  255.0 355.1 %reduce-scatter.3.cloned.1.call-start = ((), (), s32[]{:S(2)}) async-start(), calls=%async_computation.2 | async-start | bytes 7798784 | tf_op jit(solution)/shard_map/reduce_scatter | solution.py:78
  255.0 9.5 %slice-start = ((s8[7340032]{0:T(1024)(128)(4,1)}), s8[4194304]{0:T(1024)(128)(4,1)S(1)}, s32[]{:S(2)}) async-start(s8[7340032]{0:T(1024)(128)(4,1)} %bitcast.189), calls=%async_computation.5 | async-start | bytes 8388608
  256.3 8.2 %slice-start.1 = ((s8[7340032]{0:T(1024)(128)(4,1)}), s8[3145728]{0:T(1024)(128)(4,1)S(1)}, s32[]{:S(2)}) async-start(s8[7340032]{0:T(1024)(128)(4,1)} %bitcast.189), calls=%async_computation.6 | async-start | bytes 6291456
  256.3 8.2 %collective-permute-start = (bf16[32,7168]{1,0:T(8,128)(2,1)S(1)}, bf16[32,7168]{1,0:T(8,128)(2,1)S(1)}, u32[]{:S(2)}, u32[]{:S(2)}) collective-permute-start(bf16[32,7168]{1,0:T(8,128)(2,1)S(1)} %get-tuple-element.17), channel_id=1, source_target_pairs={{16,0},{32,16},{48,32},{64,48},{80,64},{96,80},{112,96},{128,112},... | collective-permute-start | bytes 1376264 | tf_op jit(solution)/shard_map/ppermute | solution.py:22
  424.8 2.0 collective-permute-start.14
  426.8 12.6 %collective-permute-start.15 = (bf16[2,448,256]{2,1,0:T(8,128)(2,1)S(1)}, bf16[2,448,256]{2,1,0:T(8,128)(2,1)S(1)}, u32[]{:S(2)}, u32[]{:S(2)}) collective-permute-start(bf16[2,448,256]{2,1,0:T(8,128)(2,1)S(1)} %collective-permute-done.14), channel_id=1, source_target_pairs={{0,32},{32,0},{16,48},{48,16},{64,96},{96,64},{80,112},{112,80},{1... | collective-permute-start | bytes 1376264 | tf_op jit(solution)/shard_map/ppermute | solution.py:16
  439.4 15.4 %collective-permute-start.16 = (bf16[2,448,256]{2,1,0:T(8,128)(2,1)S(1)}, bf16[2,448,256]{2,1,0:T(8,128)(2,1)S(1)}, u32[]{:S(2)}, u32[]{:S(2)}) collective-permute-start(bf16[2,448,256]{2,1,0:T(8,128)(2,1)S(1)} %collective-permute-done.15), channel_id=1, source_target_pairs={{0,64},{64,0},{16,80},{80,16},{32,96},{96,32},{48,112},{112,48},{1... | collective-permute-start | bytes 1376264 | tf_op jit(solution)/shard_map/ppermute | solution.py:16
  454.8 155.3 %collective-permute-start.17 = (bf16[2,448,256]{2,1,0:T(8,128)(2,1)S(1)}, bf16[2,448,256]{2,1,0:T(8,128)(2,1)S(1)}, u32[]{:S(2)}, u32[]{:S(2)}) collective-permute-start(bf16[2,448,256]{2,1,0:T(8,128)(2,1)S(1)} %collective-permute-done.16), channel_id=1, source_target_pairs={{0,128},{128,0},{16,144},{144,16},{32,160},{160,32},{48,176},{176,... | collective-permute-start | bytes 1376264 | tf_op jit(solution)/shard_map/ppermute | solution.py:16
Sparse Core Ops, SparseCore 0:
  54.8 173.5 all-gather.1
  255.1 169.6 reduce-scatter.4
  427.4 182.6 reduce-scatter.2
where the time goes:
time: 620 us; the launch traced here: 619 us
  waiting for transfers between devices  517 us (83%)
  starting transfers between devices  41.2 us (7%)
  matrix products  30.8 us (5%)
  other arithmetic  13.9 us (2%)
  between operations  13.4 us (2%)
    reduce_scatter x1, waiting for transfers between devices, per_device(): lax.psum_scatter((down_first + down_second).astype(jnp.bfloat16), 'dp', s...  154 us
    reduce_scatter x1, waiting for transfers between devices, per_device(): lax.psum_scatter((up_first + up_second).astype(jnp.bfloat16), 'dp', scatt...  153 us
    all_gather x1, waiting for transfers between devices, per_device(): other = lax.all_gather(other_piece, 'dp', axis=1, tiled=True)  132 us
    ppermute x16, waiting for transfers between devices, from_partner(): return lax.ppermute(block, axis, route)  70 us
    ppermute x16, starting transfers between devices, from_partner(): return lax.ppermute(block, axis, route)  36.7 us
  transfers between devices with their start and end apart: 21, of which 16 were waited for; matrix products, arithmetic and copies ran while one was open for 4% of the time, Pallas kernels for 0%

commit v1 on v0

v1 whole, which is shorter than its diff:
```python
import jax
import jax.numpy as jnp
from jax import lax
from jax.sharding import PartitionSpec as P

EPS = 1e-06


def contract(left, right):
    return lax.dot_general(
        left, right, (((0,), (0,)), ((), ())), preferred_element_type=jnp.float32
    )


def micro(inputs, incoming, pair, gain_in, gain_lat, need_input):
    xf = inputs.astype(jnp.float32)
    inv_in = lax.rsqrt(jnp.mean(xf * xf, axis=-1, keepdims=True) + EPS)
    normed = (xf * inv_in * gain_in.astype(jnp.float32)).astype(jnp.bfloat16)
    latent = jnp.dot(normed, pair[0], preferred_element_type=jnp.float32)
    inv_lat = lax.rsqrt(jnp.mean(latent * latent, axis=-1, keepdims=True) + EPS)
    keyed = (latent * inv_lat * gain_lat.astype(jnp.float32)).astype(jnp.bfloat16)
    dkey = jnp.dot(incoming, pair[1], preferred_element_type=jnp.float32)
    scaled = dkey * gain_lat.astype(jnp.float32)
    dlat = (
        inv_lat
        * (scaled - latent * inv_lat * inv_lat * jnp.mean(scaled * latent, axis=-1, keepdims=True))
    ).astype(jnp.bfloat16)
    result = None
    if need_input:
        dnorm = lax.dot_general(
            dlat, pair[0], (((1,), (1,)), ((), ())), preferred_element_type=jnp.float32
        )
        vgrad = dnorm * gain_in.astype(jnp.float32)
        result = (
            incoming.astype(jnp.float32)
            + inv_in * (vgrad - xf * inv_in * inv_in * jnp.mean(vgrad * xf, axis=-1, keepdims=True))
        ).astype(jnp.bfloat16)
    return result, normed, keyed, dlat


def per_device(weights, gain_model, gain_latent, saved_down, saved_up, grad_start):
    ranks = lax.axis_size("pipe")
    own = weights[0]
    own_in = gain_model[0]
    own_lat = gain_latent[0]
    mirror = [(i, ranks - 1 - i) for i in range(ranks)]
    up_x0 = lax.ppermute(saved_up[0, 0], "pipe", mirror)
    up_y0 = lax.ppermute(grad_start[1, 0], "pipe", mirror)
    up_x1 = lax.ppermute(saved_up[0, 1], "pipe", mirror)
    behind = [(i, i - 1) for i in range(1, ranks)]
    down_y0 = grad_start[0, 0]
    down_z, n_d0, k_d0, q_d0 = micro(saved_down[0, 0], down_y0, own, own_in, own_lat, True)
    down_y1 = lax.ppermute(down_z, "pipe", behind)
    up_z, n_u0, k_u0, q_u0 = micro(up_x0, up_y0, own, own_in, own_lat, True)
    up_y1 = lax.ppermute(up_z, "pipe", behind)
    _, n_d1, k_d1, q_d1 = micro(saved_down[0, 1], down_y1, own, own_in, own_lat, False)
    _, n_u1, k_u1, q_u1 = micro(up_x1, up_y1, own, own_in, own_lat, False)
    n = jnp.concatenate([n_d0, n_u0, n_d1, n_u1], axis=0)
    q = jnp.concatenate([q_d0, q_u0, q_d1, q_u1], axis=0)
    y = jnp.concatenate([down_y0, up_y0, down_y1, up_y1], axis=0)
    k = jnp.concatenate([k_d0, k_u0, k_d1, k_u1], axis=0)
    terms = jnp.stack([contract(n, q), contract(y, k)]).astype(jnp.bfloat16)
    total = lax.psum_scatter(terms, "dp", scatter_dimension=1, tiled=True)
    return total.astype(jnp.bfloat16)[None]


def solution(mesh):
    placed = (
        P("pipe", None, None, None),
        P("pipe", None),
        P("pipe", None),
        P("pipe", None, "dp", None),
        P("pipe", None, "dp", None),
        P(None, "pipe", "dp", None),
    )
    return jax.shard_map(
        per_device,
        mesh=mesh,
        in_specs=placed,
        out_specs=P("pipe", None, "dp", None),
        check_vma=False,
    )
```

time: 620 us -> 284 us (0.46)
  waiting for transfers between devices: 517 us -> 207 us
  matrix products: 30.8 us -> 15.8 us
  other arithmetic: 13.9 us -> 5.68 us
    all_gather x1 -> x0, waiting for transfers between devices: 132 us -> none  [per_device(): other = lax.all_gather(other_piece, 'dp', axis=1, tiled=True)]
    reduce_scatter x2 -> x1, waiting for transfers between devices: 307 us -> 182 us  [per_device(): total = lax.psum_scatter(terms, 'dp', scatter_dimension=1, tiled=True)]
    ppermute x18 -> x5, waiting for transfers between devices: 77.6 us -> 24.6 us  [the longest x1 10.2 us: per_device(): up_y0 = lax.ppermute(grad_start[1, 0], 'pipe', mirror)]
    convert_element_type x3 -> x1, other arithmetic: 7.99 us -> 0.09 us  [micro(): (latent * inv_lat * gain_lat.astype(jnp.float32)).astype(jnp.bfloat16)]
    dot_general x8 -> x2, matrix products: 9.72 us -> 2.29 us  [contract(): lax.dot_general(left, right, (((0,), (0,)), ((), ())), preferred_element_...]
    ppermute x18 -> x5, starting transfers between devices: 41.1 us -> 38.5 us  [the longest x1 22.3 us: per_device(): up_y1 = lax.ppermute(up_z, 'pipe', behind)]
  transfers between devices with their start and end apart: 21 -> 6, of which waited for: 16 -> 4; matrix products, arithmetic and copies ran while one was open for 4% -> 5% of each run, Pallas kernels for 0% -> 0%
where the time goes in v1:
time: 284 us; the launch traced here: 283 us
  waiting for transfers between devices  207 us (73%)
  starting transfers between devices  38.5 us (14%)
  matrix products  15.8 us (6%)
  between operations  13.6 us (5%)
  other arithmetic  5.68 us (2%)
    reduce_scatter x1, waiting for transfers between devices, per_device(): total = lax.psum_scatter(terms, 'dp', scatter_dimension=1, tiled=True)  182 us
    ppermute x1, starting transfers between devices, per_device(): up_y1 = lax.ppermute(up_z, 'pipe', behind)  22.3 us
    ppermute x1, waiting for transfers between devices, per_device(): up_y0 = lax.ppermute(grad_start[1, 0], 'pipe', mirror)  10.2 us
    ppermute x1, waiting for transfers between devices, per_device(): up_x0 = lax.ppermute(saved_up[0, 0], 'pipe', mirror)  9.11 us
    ppermute x1, starting transfers between devices, per_device(): up_x1 = lax.ppermute(saved_up[0, 1], 'pipe', mirror)  6.37 us
    ppermute x1, starting transfers between devices, per_device(): up_y0 = lax.ppermute(grad_start[1, 0], 'pipe', mirror)  6.37 us
  transfers between devices with their start and end apart: 6, of which 4 were waited for; matrix products, arithmetic and copies ran while one was open for 5% of the time, Pallas kernels for 0%

profile of v1, /device:TPU:24, one launch (start us, length us, event | category | flops | bytes accessed | tf_op | source)
XLA Modules:
  0.0 282.9 jit_solution(5509967979239118259)
XLA Ops:
  6.5 0.0 copy-start
  6.5 0.0 copy-start.1
  6.5 0.0 copy-start.4
  6.5 0.0 copy-start.3
  6.5 0.0 reduce-scatter.2.cloned.1.call-start
  6.6 1.3 slice_bitcast_fusion.2
  7.9 6.4 %collective-permute-start.1 = (bf16[32,7168]{1,0:T(8,128)(2,1)S(1)}, bf16[32,7168]{1,0:T(8,128)(2,1)S(1)}, u32[]{:S(2)}, u32[]{:S(2)}) collective-permute-start(bf16[32,7168]{1,0:T(8,128)(2,1)S(1)} %get-tuple-element.18), channel_id=1, source_target_pairs={{0,240},{16,224},{32,208},{48,192},{64,176},{80,160},{96,144},{112... | collective-permute-start | bytes 1376264 | tf_op jit(solution)/shard_map/ppermute | solution.py:49
  14.3 1.5 collective-permute-start
  15.8 1.2 slice_bitcast_fusion.1
  17.0 6.4 %collective-permute-start.2 = (bf16[32,7168]{1,0:T(8,128)(2,1)S(1)}, bf16[32,7168]{1,0:T(8,128)(2,1)S(1)}, u32[]{:S(2)}, u32[]{:S(2)}) collective-permute-start(bf16[32,7168]{1,0:T(8,128)(2,1)S(1)} %get-tuple-element.21), channel_id=1, source_target_pairs={{0,240},{16,224},{32,208},{48,192},{64,176},{80,160},{96,144},{112... | collective-permute-start | bytes 1376264 | tf_op jit(solution)/shard_map/ppermute | solution.py:48
  23.4 0.0 copy-done.1
  23.4 0.2 fusion.80
  23.6 0.0 copy-done.4
  23.6 0.0 copy-done.3
  23.7 0.0 copy-done
  23.7 0.0 copy-start.2
  23.7 2.9 %fusion.49 = f32[32,256]{1,0:T(8,128)S(1)} fusion(bf16[1,2,7168,256]{3,2,1,0:T(8,128)(2,1)} %param.6, f32[256]{0:T(256)S(1)} %bitcast.120, bf16[2,1,32,7168]{3,2,1,0:T(8,128)(2,1)S(1)} %copy-done), kind=kOutput, calls=%fused_computation.63 | convolution fusion | flops 117448704 | bytes 4162560 | tf_op jit(solution)/shard_map/dot_general | solution.py:22
  26.6 3.2 %multiply_reduce_fusion.7 = (f32[32]{0:T(128)S(1)}, f32[32]{0:T(128)S(1)}, f32[32,256]{1,0:T(8,128)S(1)}) fusion(f32[32,256]{1,0:T(8,128)S(1)} %fusion.49, bf16[1,2,7168,256]{3,2,1,0:T(8,128)(2,1)} %param.6, f32[7168]{0:T(1024)S(1)} %bitcast.115, f32[32]{0:T(128)S(1)} %add_rsqrt_fusion.7, bf16[1,2,32,7168]{3,2,1,0:T(8,128)(2,1)S(1)} %copy-done.1), kind=kOutput, calls=%fused_computation.138 | convolution fusion | flops 118390720 | bytes 4223744 | tf_op jit(solution)/shard_map/dot_general | solution.py:19
  29.8 0.1 multiply_convert_fusion.3
  29.9 0.0 copy-done.2
  29.9 1.3 fusion.84
  31.3 0.8 fusion.14
  32.1 0.0 collective-permute-done.1
  32.1 0.2 fusion.77
  32.3 9.1 %collective-permute-done = bf16[32,7168]{1,0:T(8,128)(2,1)S(1)} collective-permute-done((bf16[32,7168]{1,0:T(8,128)(2,1)S(1)}, bf16[32,7168]{1,0:T(8,128)(2,1)S(1)}, u32[]{:S(2)}, u32[]{:S(2)}) %collective-permute-start) | collective-permute-done | bytes 458784 | tf_op jit(solution)/shard_map/ppermute | solution.py:47
  41.4 0.2 fusion.89
  41.7 0.7 fusion.71
  42.4 1.9 collective-permute-start.3
  44.3 10.2 %collective-permute-done.2 = bf16[32,7168]{1,0:T(8,128)(2,1)S(1)} collective-permute-done((bf16[32,7168]{1,0:T(8,128)(2,1)S(1)}, bf16[32,7168]{1,0:T(8,128)(2,1)S(1)}, u32[]{:S(2)}, u32[]{:S(2)}) %collective-permute-start.2) | collective-permute-done | bytes 458784 | tf_op jit(solution)/shard_map/ppermute | solution.py:48
  54.5 0.7 fusion.52
  55.2 0.9 multiply_reduce_fusion.5
  56.1 0.0 collective-permute-done.3
  56.1 0.8 multiply_reduce_fusion.2
  57.0 0.1 multiply_convert_fusion.5
  57.1 1.3 fusion.90
  58.4 0.3 fusion.70
  58.7 22.3 %collective-permute-start.4 = (bf16[32,7168]{1,0:T(8,128)(2,1)S(1)}, bf16[32,7168]{1,0:T(8,128)(2,1)S(1)}, u32[]{:S(2)}, u32[]{:S(2)}) collective-permute-start(bf16[32,7168]{1,0:T(8,128)(2,1)S(1)} %fusion.70), channel_id=1, source_target_pairs={{16,0},{32,16},{48,32},{64,48},{80,64},{96,80},{112,96},{128,112},... | collective-permute-start | bytes 1376264 | tf_op jit(solution)/shard_map/ppermute | solution.py:55
  81.1 0.7 fusion.11
  81.8 5.2 %collective-permute-done.4 = bf16[32,7168]{1,0:T(8,128)(2,1)S(1)} collective-permute-done((bf16[32,7168]{1,0:T(8,128)(2,1)S(1)}, bf16[32,7168]{1,0:T(8,128)(2,1)S(1)}, u32[]{:S(2)}, u32[]{:S(2)}) %collective-permute-start.4) | collective-permute-done | bytes 458784 | tf_op jit(solution)/shard_map/ppermute | solution.py:55
  87.1 0.8 multiply_reduce_fusion
  87.9 0.1 multiply_convert_fusion.4
  88.0 1.1 fusion
  89.2 1.1 fusion.1
  90.3 3.6 %pad_maximum_fusion = bf16[2,7168,256]{2,1,0:T(8,128)(2,1)} fusion(bf16[1,7168,256]{2,1,0:T(8,128)(2,1)S(1)} %fusion.1, bf16[1,7168,256]{2,1,0:T(8,128)(2,1)S(1)} %fusion), kind=kLoop, calls=%fused_computation.6 | loop fusion | flops 3670016 | bytes 14680064 | tf_op jit(solution)/shard_map/stack | solution.py:62
  93.9 0.0 reduce-scatter.2.cloned.1.call-update
  93.9 182.1 %reduce-scatter.2.cloned.1.call-done = bf16[2,448,256]{2,1,0:T(8,128)(2,1)} async-done(((bf16[2,7168,256]{2,1,0:T(8,128)(2,1)}), bf16[2,448,256]{2,1,0:T(8,128)(2,1)}) %reduce-scatter.2.cloned.1.call-update) | async-done | bytes 458768 | tf_op jit(solution)/shard_map/reduce_scatter | solution.py:63
  (15 shorter events, 0.1 us)
Async XLA Ops:
  6.5 17.1 %copy-start = (bf16[2,1,32,7168]{3,2,1,0:T(8,128)(2,1)S(1)}, bf16[2,1,32,7168]{3,2,1,0:T(8,128)(2,1)}, u32[]{:S(2)}) copy-start(bf16[2,1,32,7168]{3,2,1,0:T(8,128)(2,1)} %param.11) | copy-start | bytes 2752516
  6.5 16.8 %copy-start.1 = (bf16[1,2,32,7168]{3,2,1,0:T(8,128)(2,1)S(1)}, bf16[1,2,32,7168]{3,2,1,0:T(8,128)(2,1)}, u32[]{:S(2)}) copy-start(bf16[1,2,32,7168]{3,2,1,0:T(8,128)(2,1)} %param.9) | copy-start | bytes 2752516
  6.5 17.1 %copy-start.4 = (bf16[1,256]{1,0:T(2,128)(2,1)S(1)}, bf16[1,256]{1,0:T(2,128)(2,1)}, u32[]{:S(2)}) copy-start(bf16[1,256]{1,0:T(2,128)(2,1)} %param.8) | copy-start | bytes 1540
  6.5 17.1 %copy-start.3 = (bf16[1,7168]{1,0:T(2,128)(2,1)S(1)}, bf16[1,7168]{1,0:T(2,128)(2,1)}, u32[]{:S(2)}) copy-start(bf16[1,7168]{1,0:T(2,128)(2,1)} %param.7) | copy-start | bytes 43012
  6.5 269.5 %reduce-scatter.2.cloned.1.call-start = ((), (), s32[]{:S(2)}) async-start(), calls=%async_computation.1 | async-start | bytes 7798784 | tf_op jit(solution)/shard_map/reduce_scatter | solution.py:63
  7.9 24.1 %collective-permute-start.1 = (bf16[32,7168]{1,0:T(8,128)(2,1)S(1)}, bf16[32,7168]{1,0:T(8,128)(2,1)S(1)}, u32[]{:S(2)}, u32[]{:S(2)}) collective-permute-start(bf16[32,7168]{1,0:T(8,128)(2,1)S(1)} %get-tuple-element.18), channel_id=1, source_target_pairs={{0,240},{16,224},{32,208},{48,192},{64,176},{80,160},{96,144},{112... | collective-permute-start | bytes 1376264 | tf_op jit(solution)/shard_map/ppermute | solution.py:49
  14.3 27.1 %collective-permute-start = (bf16[32,7168]{1,0:T(8,128)(2,1)S(1)}, bf16[32,7168]{1,0:T(8,128)(2,1)S(1)}, u32[]{:S(2)}, u32[]{:S(2)}) collective-permute-start(bf16[32,7168]{1,0:T(8,128)(2,1)S(1)} %get-tuple-element.19), channel_id=1, source_target_pairs={{0,240},{16,224},{32,208},{48,192},{64,176},{80,160},{96,144},{112... | collective-permute-start | bytes 1376264 | tf_op jit(solution)/shard_map/ppermute | solution.py:47
  17.0 37.5 %collective-permute-start.2 = (bf16[32,7168]{1,0:T(8,128)(2,1)S(1)}, bf16[32,7168]{1,0:T(8,128)(2,1)S(1)}, u32[]{:S(2)}, u32[]{:S(2)}) collective-permute-start(bf16[32,7168]{1,0:T(8,128)(2,1)S(1)} %get-tuple-element.21), channel_id=1, source_target_pairs={{0,240},{16,224},{32,208},{48,192},{64,176},{80,160},{96,144},{112... | collective-permute-start | bytes 1376264 | tf_op jit(solution)/shard_map/ppermute | solution.py:48
  23.7 6.2 %copy-start.2 = (bf16[1,2,7168,256]{3,2,1,0:T(8,128)(2,1)S(1)}, bf16[1,2,7168,256]{3,2,1,0:T(8,128)(2,1)}, u32[]{:S(2)}) copy-start(bf16[1,2,7168,256]{3,2,1,0:T(8,128)(2,1)} %param.6) | copy-start | bytes 22020100
  42.4 13.8 %collective-permute-start.3 = (bf16[32,7168]{1,0:T(8,128)(2,1)S(1)}, bf16[32,7168]{1,0:T(8,128)(2,1)S(1)}, u32[]{:S(2)}, u32[]{:S(2)}) collective-permute-start(bf16[32,7168]{1,0:T(8,128)(2,1)S(1)} %get-tuple-element.17), channel_id=1, source_target_pairs={{16,0},{32,16},{48,32},{64,48},{80,64},{96,80},{112,96},{128,112},... | collective-permute-start | bytes 1376264 | tf_op jit(solution)/shard_map/ppermute | solution.py:53
  58.7 28.3 %collective-permute-start.4 = (bf16[32,7168]{1,0:T(8,128)(2,1)S(1)}, bf16[32,7168]{1,0:T(8,128)(2,1)S(1)}, u32[]{:S(2)}, u32[]{:S(2)}) collective-permute-start(bf16[32,7168]{1,0:T(8,128)(2,1)S(1)} %fusion.70), channel_id=1, source_target_pairs={{16,0},{32,16},{48,32},{64,48},{80,64},{96,80},{112,96},{128,112},... | collective-permute-start | bytes 1376264 | tf_op jit(solution)/shard_map/ppermute | solution.py:55
Sparse Core Ops, SparseCore 0:
  94.1 181.9 reduce-scatter.1

commit v2 on v1

v2 whole, which is shorter than its diff:
```python
import jax
import jax.numpy as jnp
from jax import lax
from jax.experimental import pallas as pl
from jax.experimental.pallas import tpu as pltpu
from jax.sharding import PartitionSpec as P

EPS = 1e-06
MESH = pl.DeviceIdType.MESH
BF = jnp.bfloat16
F32 = jnp.float32
X = 4
Z = 4
CHUNK = 1024


def kernel(w_hbm, sd_hbm, su_hbm, gs_hbm, gm_ref, gl_ref, out_ref,
           w, xr, yr, xg, zr, xq, yq, ak, acc, sb, rb, kept,
           lsem, bsem_s, bsem_r, rsem_s, rsem_r, xs_s, xs_r, zs_s, zs_r):
    pipe = lax.axis_index("pipe")
    dp = lax.axis_index("dp")
    ranks = lax.axis_size("pipe")
    x = dp // Z
    z = lax.rem(dp, Z)
    rows, width = xr.shape[1], xr.shape[2]
    quarter = width // X
    block = quarter // Z
    lat = w.shape[2]
    chunks = width // CHUNK

    loads = []
    for i, (src, dst) in enumerate([
        (sd_hbm.at[0, 0], xr.at[0]), (w_hbm.at[0, 0], w.at[0]), (gs_hbm.at[0, 0], yr.at[0]),
        (w_hbm.at[0, 1], w.at[1]), (sd_hbm.at[0, 1], xr.at[2]),
    ]):
        c = pltpu.make_async_copy(src, dst, lsem.at[i])
        c.start()
        loads.append(c)

    mirror = {"pipe": ranks - 1 - pipe, "dp": x * Z + lax.rem(z + 2, Z)}
    xpeer = [{"pipe": pipe, "dp": lax.rem(x + k, X) * Z + z} for k in range(1, X)]
    zpeer = [{"pipe": pipe, "dp": x * Z + lax.rem(z + k, Z)} for k in range(1, Z)]
    before = {"pipe": lax.rem(pipe + ranks - 1, ranks), "dp": dp}
    after = {"pipe": lax.rem(pipe + 1, ranks), "dp": dp}
    barrier = pltpu.get_barrier_semaphore()
    greet = [mirror, before, after] + xpeer + zpeer
    for d in greet:
        pl.semaphore_signal(barrier, inc=1, device_id=d, device_id_type=MESH)
    pl.semaphore_wait(barrier, len(greet))

    def remote(src, dst, ss, rs, dev):
        return pltpu.make_async_remote_copy(
            src_ref=src, dst_ref=dst, send_sem=ss, recv_sem=rs, device_id=dev, device_id_type=MESH)

    up_x0 = remote(su_hbm.at[0, 0], xr.at[1], bsem_s.at[0], bsem_r.at[0], mirror)
    up_y0 = remote(gs_hbm.at[1, 0], yr.at[1], bsem_s.at[1], bsem_r.at[1], mirror)
    up_x1 = remote(su_hbm.at[0, 1], xr.at[3], bsem_s.at[2], bsem_r.at[2], mirror)
    up_x0.start()
    up_y0.start()

    h = gl_ref[...].astype(F32)
    tokens = pl.ds(pl.multiple_of(x * rows, rows), rows)
    mine = pl.ds(pl.multiple_of(x * quarter, 128), quarter)

    def phase_c(m):
        def body(i, carry):
            ss, total = carry
            cols = pl.ds(pl.multiple_of(i * CHUNK, CHUNK), CHUNK)
            xf = xr[m, :, cols].astype(F32)
            ss = ss + jnp.sum(xf * xf, axis=-1, keepdims=True)
            g = (xf * gm_ref[:, cols].astype(F32)).astype(BF)
            xg[m, :, cols] = g
            total = total + jnp.dot(g, w[0, cols, :], preferred_element_type=F32)
            return ss, total
        ss, total = lax.fori_loop(
            0, chunks, body, (jnp.zeros((rows, 1), F32), jnp.zeros((rows, lat), F32)))
        a = lax.rsqrt(ss / width + EPS)
        c = total * a
        b = lax.rsqrt(jnp.mean(c * c, axis=-1, keepdims=True) + EPS)
        ak[m, tokens, pl.ds(lat, lat)] = (c * b * h).astype(BF)
        return a, b, c, total

    def phase_e(m, state):
        a, b, c, total = state
        def body(i, e):
            cols = pl.ds(pl.multiple_of(i * CHUNK, CHUNK), CHUNK)
            return e + jnp.dot(yr[m, :, cols], w[1, cols, :], preferred_element_type=F32)
        e = lax.fori_loop(0, chunks, body, jnp.zeros((rows, lat), F32))
        u = e * h
        q = b * (u - c * b * b * jnp.mean(u * c, axis=-1, keepdims=True))
        ak[m, tokens, pl.ds(0, lat)] = (a * q).astype(BF)
        return q.astype(BF)

    def phase_z(m, slot, state, q):
        a, b, c, total = state
        mean = jnp.sum(total * q.astype(F32), axis=-1, keepdims=True) / width
        scale = a * a * mean
        def body(i, carry):
            cols = pl.ds(pl.multiple_of(i * CHUNK, CHUNK), CHUNK)
            v = lax.dot_general(q, w[0, cols, :], (((1,), (1,)), ((), ())), preferred_element_type=F32)
            v = v * gm_ref[:, cols].astype(F32)
            zz = yr[m, :, cols].astype(F32) + a * (v - xr[m, :, cols].astype(F32) * scale)
            zr[slot, :, cols] = zz.astype(BF)
            return carry
        lax.fori_loop(0, chunks, body, 0)

    pending = []

    def spread(what, m):
        out = []
        for k in range(1, X):
            far = pl.ds(pl.multiple_of(lax.rem(x + k, X) * quarter, 128), quarter)
            if what == 0:
                src, dst = xg.at[m, :, far], xq.at[m, tokens, :]
            elif what == 1:
                src, dst = yr.at[m, :, far], yq.at[m, tokens, :]
            else:
                src, dst = ak.at[m, tokens, :], ak.at[m, tokens, :]
            c = remote(src, dst, xs_s.at[what, m, k - 1], xs_r.at[what, m, k - 1], xpeer[k - 1])
            c.start()
            out.append(c)
        if what == 0:
            xq[m, tokens, :] = xg[m, :, mine]
        elif what == 1:
            yq[m, tokens, :] = yr[m, :, mine]
        pending.append((m, out))

    def relay(slot, m):
        return remote(zr.at[slot], yr.at[m], rsem_s.at[slot], rsem_r.at[slot], before)

    def gather(m):
        for mm, cs in pending:
            if mm == m:
                for c in cs:
                    c.wait_recv()

    def grads(m, first):
        def body(i, carry):
            cols = pl.ds(pl.multiple_of(i * 256, 256), 256)
            for half, src in ((0, xq), (1, yq)):
                t = lax.dot_general(src[m, :, cols], ak[m, :, pl.ds(half * lat, lat)],
                                    (((0,), (0,)), ((), ())), preferred_element_type=F32)
                if first:
                    acc[half, cols, :] = t
                else:
                    acc[half, cols, :] += t
            return carry
        lax.fori_loop(0, quarter // 256, body, 0)

    loads[0].wait()
    loads[1].wait()
    s0 = phase_c(0)
    spread(0, 0)
    loads[2].wait()
    loads[3].wait()
    spread(1, 0)
    q0 = phase_e(0, s0)
    spread(2, 0)
    phase_z(0, 0, s0, q0)
    down = relay(0, 2)

    @pl.when(pipe > 0)
    def _():
        down.start()

    loads[4].wait()
    s2 = phase_c(2)
    spread(0, 2)

    up_x0.wait_send()
    up_y0.wait_send()
    up_x1.start()
    up_x0.wait_recv()
    s1 = phase_c(1)
    up_y0.wait_recv()
    q1 = phase_e(1, s1)
    phase_z(1, 1, s1, q1)
    up = relay(1, 3)

    @pl.when(pipe > 0)
    def _():
        up.start()

    spread(0, 1)
    spread(1, 1)
    spread(2, 1)
    gather(0)
    grads(0, True)

    @pl.when(pipe < ranks - 1)
    def _():
        down.wait_recv()

    @pl.when(pipe == ranks - 1)
    def _():
        yr[2] = jnp.zeros((rows, width), BF)
        yr[3] = jnp.zeros((rows, width), BF)

    spread(1, 2)
    phase_e(2, s2)
    spread(2, 2)
    up_x1.wait_recv()
    s3 = phase_c(3)
    spread(0, 3)
    gather(1)
    grads(1, False)
    gather(2)
    grads(2, False)

    @pl.when(pipe < ranks - 1)
    def _():
        up.wait_recv()

    spread(1, 3)
    phase_e(3, s3)
    spread(2, 3)
    gather(3)
    grads(3, False)

    sends = []
    for k in (2, 1, 3):
        far = pl.ds(pl.multiple_of(lax.rem(z + k, Z) * block, 16), block)
        sb[k - 1] = acc[:, far, :].astype(BF)
        c = remote(sb.at[k - 1], rb.at[k - 1], zs_s.at[k - 1], zs_r.at[k - 1], zpeer[k - 1])
        c.start()
        sends.append(c)
    near = pl.ds(pl.multiple_of(z * block, 16), block)
    total = acc[:, near, :].astype(BF).astype(F32)
    for c in sends:
        c.wait_recv()
    for k in range(1, Z):
        total = total + rb[k - 1].astype(F32)
    out_ref[...] = total.astype(BF)

    for c in sends:
        c.wait_send()
    for mm, cs in pending:
        for c in cs:
            c.wait_send()
    up_x1.wait_send()

    @pl.when(pipe > 0)
    def _():
        down.wait_send()
        up.wait_send()


def per_device(weights, gain_model, gain_latent, saved_down, saved_up, grad_start):
    _, _, width, lat = weights.shape
    rows = saved_down.shape[2]
    quarter = width // X
    block = quarter // Z
    dma = pltpu.SemaphoreType.DMA
    any_spec = pl.BlockSpec(memory_space=pl.ANY)
    vmem = pl.BlockSpec(memory_space=pltpu.VMEM)
    out = pl.pallas_call(
        kernel,
        out_shape=jax.ShapeDtypeStruct((2, block, lat), BF),
        in_specs=[any_spec] * 4 + [vmem] * 2,
        out_specs=vmem,
        scratch_shapes=[
            pltpu.VMEM((2, width, lat), BF),
            pltpu.VMEM((4, rows, width), BF),
            pltpu.VMEM((4, rows, width), BF),
            pltpu.VMEM((4, rows, width), BF),
            pltpu.VMEM((2, rows, width), BF),
            pltpu.VMEM((4, X * rows, quarter), BF),
            pltpu.VMEM((4, X * rows, quarter), BF),
            pltpu.VMEM((4, X * rows, 2 * lat), BF),
            pltpu.VMEM((2, quarter, lat), F32),
            pltpu.VMEM((3, 2, block, lat), BF),
            pltpu.VMEM((3, 2, block, lat), BF),
            pltpu.VMEM((8, 128), F32),
            dma((5,)),
            dma((3,)), dma((3,)),
            dma((2,)), dma((2,)),
            dma((3, 4, 3)), dma((3, 4, 3)),
            dma((3,)), dma((3,)),
        ],
        compiler_params=pltpu.CompilerParams(
            collective_id=0, has_side_effects=True, vmem_limit_bytes=56 << 20),
        name="relay_step",
    )(weights, saved_down, saved_up, grad_start, gain_model, gain_latent)
    return out[None]


def solution(mesh):
    placed = (
        P("pipe", None, None, None),
        P("pipe", None),
        P("pipe", None),
        P("pipe", None, "dp", None),
        P("pipe", None, "dp", None),
        P(None, "pipe", "dp", None),
    )
    return jax.shard_map(
        per_device,
        mesh=mesh,
        in_specs=placed,
        out_specs=P("pipe", None, "dp", None),
        check_vma=False,
    )
```

time: 284 us -> 142 us (0.50)
  waiting for transfers between devices: 207 us -> 0 us
  Pallas kernels: 0 us -> 140 us
  starting transfers between devices: 38.5 us -> 0 us
  matrix products: 15.8 us -> 0 us
  between operations: 13.6 us -> 0.01 us
  other arithmetic: 5.68 us -> 0 us
    reduce_scatter x1 -> x0, waiting for transfers between devices: 182 us -> none  [per_device(): total = lax.psum_scatter(terms, 'dp', scatter_dimension=1, tiled=True)]
    pallas_call x0 -> x1, Pallas kernels: none -> 140 us  [per_device(): pl.pallas_call(kernel, out_shape=jax.ShapeDtypeStruct((2, block, lat), BF...]
    ppermute x5 -> x0, starting transfers between devices: 38.5 us -> none  [the longest x1 22.3 us: per_device(): up_y1 = lax.ppermute(up_z, 'pipe', behind)]
    ppermute x5 -> x0, waiting for transfers between devices: 24.6 us -> none  [the longest x1 10.2 us: per_device(): up_y0 = lax.ppermute(grad_start[1, 0], 'pipe', mirror)]
    dot_general x12 -> x0, matrix products: 15.8 us -> none  [the longest x4 5.57 us: micro(): latent = jnp.dot(normed, pair[0], preferred_element_type=jnp.float32)]
    another operation x1 -> x0, other arithmetic: 3.6 us -> none  [per_device(): terms = jnp.stack([contract(n, q), contract(y, k)]).astype(jnp.bfloat16)]
  transfers between devices with their start and end apart: 6 -> 0, of which waited for: 4 -> 0; matrix products, arithmetic and copies ran while one was open for 5% -> 0% of each run, Pallas kernels for 0% -> 0%
where the time goes in v2:
time: 142 us
  Pallas kernels  140 us (99%)
  local copies, waits for them, and re-layouts  1.82 us (1%)
    pallas_call x1, Pallas kernels, per_device(): pl.pallas_call(kernel, out_shape=jax.ShapeDtypeStruct((2, block, lat), BF...  140 us

profile of v2, /device:TPU:24, one launch (start us, length us, event | category | flops | bytes accessed | tf_op | source)
XLA Modules:
  0.0 141.8 jit_solution(5757420886995233883)
XLA Ops:
  0.0 139.9 %relay_step.1 = bf16[2,448,256]{2,1,0:T(8,128)(2,1)} custom-call(bf16[1,2,7168,256]{3,2,1,0:T(8,128)(2,1)} %w_hbm.1, bf16[1,2,32,7168]{3,2,1,0:T(8,128)(2,1)} %sd_hbm.1, bf16[1,2,32,7168]{3,2,1,0:T(8,128)(2,1)} %su_hbm.1, bf16[2,1,32,7168]{3,2,1,0:T(8,128)(2,1)} %gs_hbm.1, bf16[1,7168]{1,0:T(2,128)(2,1)} %gm_ref.1, bf16[1,256]{1,0:T(2,128)(2,1)} %gl_ref.1), custom_call_target="tpu_custom_call" | custom-call | tf_op jit(solution)/shard_map/relay_step/pallas_call | solution.py:256
  139.9 1.8 %copy.8 = bf16[1,2,448,256]{3,2,1,0:T(8,128)(2,1)} copy(bf16[1,2,448,256]{3,2,1,0:T(8,128)(2,1)} %bitcast.1) | data formatting | bytes 917504

commit v3 on v1

v3 whole, which is shorter than its diff:
```python
import jax
import jax.numpy as jnp
from jax import lax
from jax.experimental import pallas as pl
from jax.experimental.pallas import tpu as pltpu
from jax.sharding import PartitionSpec as P

EPS = 1e-06
MESH = pl.DeviceIdType.MESH
BF = jnp.bfloat16
F32 = jnp.float32
X = 4
Z = 4
STEP = 1792
UX0, UY0, DX0, DY0, UX1, DX1 = range(6)


def kernel(w_hbm, sd_hbm, su_hbm, gs_hbm, gm_ref, gl_ref, out_ref,
           raw, w, xs, xg, ys, zr, inv, pf, pb, pr, kk, qq, acc, sb, rb, via,
           lsem, in_s, in_r, a_s, a_r, rs_s, rs_r, ag_s, ag_r, rl_s, rl_r, gr_s, gr_r, via_s, via_r):
    pipe = lax.axis_index("pipe")
    dp = lax.axis_index("dp")
    ranks = lax.axis_size("pipe")
    x = dp // Z
    z = lax.rem(dp, Z)
    rows, width = raw.shape[1], raw.shape[2]
    quarter = width // X
    block = quarter // Z
    lat = w.shape[2]
    tokens = X * rows

    inputs = [su_hbm.at[0, 0], gs_hbm.at[1, 0], sd_hbm.at[0, 0], gs_hbm.at[0, 0], su_hbm.at[0, 1], sd_hbm.at[0, 1]]
    mine = pl.ds(pl.multiple_of(x * quarter, 128), quarter)
    here = pl.ds(pl.multiple_of(x * rows, rows), rows)
    raw_loads = {}
    for j, i in enumerate((UX0, DX0, UX1, DX1)):
        raw_loads[i] = (j, pltpu.make_async_copy(inputs[i], raw.at[j], lsem.at[j]))
    own_loads = {}
    for j, (i, dst) in enumerate(((DX0, xs.at[0]), (DY0, ys.at[0]), (DX1, xs.at[2]))):
        own_loads[i] = pltpu.make_async_copy(inputs[i].at[:, mine], dst.at[here], lsem.at[4 + j])
    w_loads = [pltpu.make_async_copy(w_hbm.at[0, half, mine, :], w.at[half], lsem.at[7 + half]) for half in range(2)]
    for c in [raw_loads[UX0][1], own_loads[DX0], w_loads[0], own_loads[DY0], w_loads[1],
              raw_loads[DX0][1], raw_loads[UX1][1], raw_loads[DX1][1], own_loads[DX1]]:
        c.start()

    mirror = [{"pipe": ranks - 1 - pipe, "dp": lax.rem(x + k, X) * Z + lax.rem(z + 2, Z)} for k in range(X)]
    xpeer = [{"pipe": pipe, "dp": lax.rem(x + k, X) * Z + z} for k in range(1, X)]
    zpeer = [{"pipe": pipe, "dp": x * Z + lax.rem(z + k, Z)} for k in range(1, Z)]
    before = {"pipe": lax.rem(pipe + ranks - 1, ranks), "dp": dp}
    after = {"pipe": lax.rem(pipe + 1, ranks), "dp": dp}
    barrier = pltpu.get_barrier_semaphore()
    greet = mirror + [before, after] + xpeer + zpeer
    for d in greet:
        pl.semaphore_signal(barrier, inc=1, device_id=d, device_id_type=MESH)

    def remote(src, dst, ss, rs, dev):
        return pltpu.make_async_remote_copy(
            src_ref=src, dst_ref=dst, send_sem=ss, recv_sem=rs, device_id=dev, device_id_type=MESH)

    def inverse(i):
        j, load = raw_loads[i]
        load.wait()

        def body(n, ss):
            xf = raw[j, :, pl.ds(pl.multiple_of(n * 1024, 1024), 1024)].astype(F32)
            return ss + jnp.sum(xf * xf, axis=-1, keepdims=True)
        ss = lax.fori_loop(0, width // 1024, body, jnp.zeros((rows, 1), F32))
        return jnp.broadcast_to(lax.rsqrt(ss / width + EPS), (rows, 128))

    sent = []

    def cut(i, k):
        return inputs[i].at[:, pl.ds(pl.multiple_of(lax.rem(x + k, X) * quarter, 128), quarter)]

    def send_up(i, dst):
        cs = []
        for k in range(X):
            c = remote(cut(i, k), dst.at[here], in_s.at[i, k], in_r.at[i, k], mirror[k])
            c.start()
            cs.append(c)
        return cs

    def send_down(i, dst):
        cs = []
        for k in range(1, X):
            c = remote(cut(i, k), dst.at[here], in_s.at[i, k], in_r.at[i, k], xpeer[k - 1])
            c.start()
            cs.append(c)
        sent.extend(cs)
        return cs

    pl.semaphore_wait(barrier, len(greet))
    up_x0 = send_up(UX0, xs.at[1])
    up_y0 = send_up(UY0, ys.at[1])
    down_x0 = send_down(DX0, xs.at[0])
    down_y0 = send_down(DY0, ys.at[0])
    down_x1 = send_down(DX1, xs.at[2])
    inv[4] = inverse(UX0)
    up_a0 = remote(inv.at[4], inv.at[1], a_s.at[0], a_r.at[0], mirror[0])
    up_a0.start()
    inv[0] = inverse(DX0)
    h = gl_ref[...].astype(F32)

    def arrive(cs):
        for c in cs:
            c.wait_recv()

    def reduce_start(m, which, part):
        pf[m, which] = part
        pb[m, which] = part.astype(BF)
        cs = []
        for k in range(1, Z):
            far = pl.ds(pl.multiple_of(lax.rem(x + k, X) * rows, rows), rows)
            c = remote(pb.at[m, which, far, :], pr.at[m, which, k - 1],
                       rs_s.at[m, which, k - 1], rs_r.at[m, which, k - 1], xpeer[k - 1])
            c.start()
            cs.append(c)
        sent.extend(cs)
        return cs

    def reduce_end(m, which, cs):
        arrive(cs)
        total = pf[m, which, here, :]
        for k in range(1, Z):
            total = total + pr[m, which, k - 1].astype(F32)
        return total

    def gather_start(m, which, buf):
        cs = []
        for k in range(1, Z):
            c = remote(buf.at[m, here, :], buf.at[m, here, :],
                       ag_s.at[m, which, k - 1], ag_r.at[m, which, k - 1], xpeer[k - 1])
            c.start()
            cs.append(c)
        sent.extend(cs)
        return cs

    def gain(i):
        return gm_ref[:, pl.ds(pl.multiple_of(x * quarter + i * STEP, 128), STEP)].astype(F32)

    def part_c(m):
        def body(i, total):
            cols = pl.ds(pl.multiple_of(i * STEP, STEP), STEP)
            g = (xs[m, :, cols].astype(F32) * gain(i)).astype(BF)
            xg[m, :, cols] = g
            return total + jnp.dot(g, w[0, cols, :], preferred_element_type=F32)
        part = lax.fori_loop(0, quarter // STEP, body, jnp.zeros((tokens, lat), F32))
        return reduce_start(m, 0, part)

    def part_e(m):
        def body(i, total):
            cols = pl.ds(pl.multiple_of(i * STEP, STEP), STEP)
            return total + jnp.dot(ys[m, :, cols], w[1, cols, :], preferred_element_type=F32)
        part = lax.fori_loop(0, quarter // STEP, body, jnp.zeros((tokens, lat), F32))
        return reduce_start(m, 1, part)

    def latent_k(m, cs):
        total = reduce_end(m, 0, cs)
        a = inv[m, :, 0:1]
        c = total * a
        b = lax.rsqrt(jnp.mean(c * c, axis=-1, keepdims=True) + EPS)
        kk[m, here, :] = (c * b * h).astype(BF)
        return (a, b, c, total), gather_start(m, 0, kk)

    def latent_q(m, state, cs):
        a, b, c, total = state
        u = reduce_end(m, 1, cs) * h
        q = b * (u - c * b * b * jnp.mean(u * c, axis=-1, keepdims=True))
        aq = (a * q).astype(BF)
        t = a * a * jnp.sum(total * aq.astype(F32), axis=-1, keepdims=True) / width
        qq[m, here, 0:lat] = aq
        qq[m, here, lat:lat + 128] = jnp.broadcast_to(t, (rows, 128)).astype(BF)
        return gather_start(m, 1, qq)

    def input_grad(m):
        q = qq[m, :, 0:lat]
        t = qq[m, :, lat:lat + 1].astype(F32)
        def body(i, carry):
            cols = pl.ds(pl.multiple_of(i * STEP, STEP), STEP)
            v = lax.dot_general(q, w[0, cols, :], (((1,), (1,)), ((), ())), preferred_element_type=F32)
            zz = ys[m, :, cols].astype(F32) + v * gain(i) - xs[m, :, cols].astype(F32) * t
            zr[m, :, cols] = zz.astype(BF)
            return carry
        lax.fori_loop(0, quarter // STEP, body, 0)

    def relay(m):
        return remote(zr.at[m], ys.at[m + 2], rl_s.at[m], rl_r.at[m], before)

    def grads(half, m):
        def body(i, carry):
            cols = pl.ds(pl.multiple_of(i * STEP, STEP), STEP)
            left = xg[m, :, cols] if half == 0 else ys[m, :, cols]
            right = qq[m, :, 0:lat] if half == 0 else kk[m]
            t = lax.dot_general(left, right, (((0,), (0,)), ((), ())), preferred_element_type=F32)
            if m == 0:
                acc[half, cols, :] = t
            else:
                acc[half, cols, :] += t
            return carry
        lax.fori_loop(0, quarter // STEP, body, 0)

    def far_block(k):
        return pl.ds(pl.multiple_of(lax.rem(z + k, Z) * block, 16), block)

    inner = jnp.logical_or(z == 1, z == 2)
    direct = [[remote(sb.at[half, k - 1], rb.at[half, k - 1], gr_s.at[half, k - 1], gr_r.at[half, k - 1], zpeer[k - 1])
               for k in range(1, Z)] for half in range(2)]
    ahead = [{k - 1: remote(sb.at[half, k - 1], via.at[half], via_s.at[half], via_r.at[half], zpeer[Z - k - 1])
              for k in (1, 3)} for half in range(2)]

    def blocks_start(half):
        @pl.when(z == 0)
        def _():
            for k in (3, 2, 1):
                sb[half, k - 1] = acc[half, far_block(k), :].astype(BF)
                (ahead if k == 3 else direct)[half][k - 1].start()

        @pl.when(z == 3)
        def _():
            for k in (1, 2, 3):
                sb[half, k - 1] = acc[half, far_block(k), :].astype(BF)
                (ahead if k == 1 else direct)[half][k - 1].start()

        @pl.when(inner)
        def _():
            for k in (1, 3):
                sb[half, k - 1] = acc[half, far_block(k), :].astype(BF)
                direct[half][k - 1].start()

    def blocks_pass(half):
        @pl.when(inner)
        def _():
            ahead[half][0].wait_recv()
            sb[half, 1] = (acc[half, far_block(2), :] + via[half].astype(F32)).astype(BF)
            direct[half][1].start()

    def blocks_end(half):
        near = pl.ds(pl.multiple_of(z * block, 16), block)
        total = acc[half, near, :].astype(BF).astype(F32)
        direct[half][1].wait_recv()
        total = total + rb[half, 1].astype(F32)

        @pl.when(z == 0)
        def _():
            direct[half][2].wait_recv()
            out_ref[half] = (total + rb[half, 2].astype(F32)).astype(BF)

        @pl.when(z == 3)
        def _():
            direct[half][0].wait_recv()
            out_ref[half] = (total + rb[half, 0].astype(F32)).astype(BF)

        @pl.when(inner)
        def _():
            direct[half][0].wait_recv()
            direct[half][2].wait_recv()
            out_ref[half] = (total + rb[half, 0].astype(F32) + rb[half, 2].astype(F32)).astype(BF)

    def blocks_sent(half):
        direct[half][1].wait_send()

        @pl.when(z == 0)
        def _():
            ahead[half][2].wait_send()
            direct[half][0].wait_send()

        @pl.when(z == 3)
        def _():
            ahead[half][0].wait_send()
            direct[half][2].wait_send()

        @pl.when(inner)
        def _():
            direct[half][0].wait_send()
            direct[half][2].wait_send()

    for i in (DX0, DY0):
        own_loads[i].wait()
    for c in w_loads:
        c.wait()
    arrive(down_x0)
    rc0 = part_c(0)
    arrive(down_y0)
    re0 = part_e(0)
    s0, gk0 = latent_k(0, rc0)
    gq0 = latent_q(0, s0, re0)
    arrive(gq0)
    input_grad(0)
    down = relay(0)

    @pl.when(pipe > 0)
    def _():
        down.start()

    inv[5] = inverse(UX1)
    inv[2] = inverse(DX1)
    arrive(gk0)
    grads(0, 0)
    grads(1, 0)
    own_loads[DX1].wait()
    arrive(down_x1)
    rc2 = part_c(2)
    s2, gk2 = latent_k(2, rc2)

    for c in up_x0 + up_y0:
        c.wait_send()
    up_x1 = send_up(UX1, xs.at[3])
    up_a1 = remote(inv.at[5], inv.at[3], a_s.at[1], a_r.at[1], mirror[0])
    up_a1.start()
    arrive(up_x0)
    rc1 = part_c(1)
    arrive(up_y0)
    re1 = part_e(1)
    up_a0.wait_recv()
    s1, gk1 = latent_k(1, rc1)
    gq1 = latent_q(1, s1, re1)
    arrive(gq1)
    input_grad(1)
    up = relay(1)

    @pl.when(pipe > 0)
    def _():
        up.start()

    @pl.when(pipe < ranks - 1)
    def _():
        down.wait_recv()

    @pl.when(pipe == ranks - 1)
    def _():
        ys[2] = jnp.zeros((tokens, quarter), BF)
        ys[3] = jnp.zeros((tokens, quarter), BF)

    re2 = part_e(2)
    arrive(gk1)
    grads(0, 1)
    grads(1, 1)
    gq2 = latent_q(2, s2, re2)
    arrive(gk2)
    grads(1, 2)
    arrive(gq2)
    grads(0, 2)

    arrive(up_x1)
    rc3 = part_c(3)

    @pl.when(pipe < ranks - 1)
    def _():
        up.wait_recv()

    re3 = part_e(3)
    up_a1.wait_recv()
    s3, gk3 = latent_k(3, rc3)
    gq3 = latent_q(3, s3, re3)
    arrive(gk3)
    grads(1, 3)
    blocks_start(1)
    arrive(gq3)
    grads(0, 3)
    blocks_pass(1)
    blocks_start(0)
    blocks_pass(0)
    blocks_end(1)
    blocks_end(0)
    blocks_sent(1)
    blocks_sent(0)

    for c in sent + up_x1 + [up_a0, up_a1]:
        c.wait_send()

    @pl.when(pipe > 0)
    def _():
        down.wait_send()
        up.wait_send()


def per_device(weights, gain_model, gain_latent, saved_down, saved_up, grad_start):
    _, _, width, lat = weights.shape
    rows = saved_down.shape[2]
    quarter = width // X
    block = quarter // Z
    tokens = X * rows
    dma = pltpu.SemaphoreType.DMA
    any_spec = pl.BlockSpec(memory_space=pl.ANY)
    vmem = pl.BlockSpec(memory_space=pltpu.VMEM)
    out = pl.pallas_call(
        kernel,
        out_shape=jax.ShapeDtypeStruct((2, block, lat), BF),
        in_specs=[any_spec] * 4 + [vmem] * 2,
        out_specs=vmem,
        scratch_shapes=[
            pltpu.VMEM((4, rows, width), BF),
            pltpu.VMEM((2, quarter, lat), BF),
            pltpu.VMEM((4, tokens, quarter), BF),
            pltpu.VMEM((4, tokens, quarter), BF),
            pltpu.VMEM((4, tokens, quarter), BF),
            pltpu.VMEM((2, tokens, quarter), BF),
            pltpu.VMEM((6, rows, 128), F32),
            pltpu.VMEM((4, 2, tokens, lat), F32),
            pltpu.VMEM((4, 2, tokens, lat), BF),
            pltpu.VMEM((4, 2, 3, rows, lat), BF),
            pltpu.VMEM((4, tokens, lat), BF),
            pltpu.VMEM((4, tokens, lat + 128), BF),
            pltpu.VMEM((2, quarter, lat), F32),
            pltpu.VMEM((2, 3, block, lat), BF),
            pltpu.VMEM((2, 3, block, lat), BF),
            pltpu.VMEM((2, block, lat), BF),
            dma((9,)),
            dma((6, 4)), dma((6, 4)),
            dma((2,)), dma((2,)),
            dma((4, 2, 3)), dma((4, 2, 3)),
            dma((4, 2, 3)), dma((4, 2, 3)),
            dma((2,)), dma((2,)),
            dma((2, 3)), dma((2, 3)),
            dma((2,)), dma((2,)),
        ],
        compiler_params=pltpu.CompilerParams(
            collective_id=0, has_side_effects=True, vmem_limit_bytes=56 << 20),
        name="relay_step",
    )(weights, saved_down, saved_up, grad_start, gain_model, gain_latent)
    return out[None]


def solution(mesh):
    placed = (
        P("pipe", None, None, None),
        P("pipe", None),
        P("pipe", None),
        P("pipe", None, "dp", None),
        P("pipe", None, "dp", None),
        P(None, "pipe", "dp", None),
    )
    return jax.shard_map(
        per_device,
        mesh=mesh,
        in_specs=placed,
        out_specs=P("pipe", None, "dp", None),
        check_vma=False,
    )
```

time: 284 us -> 133 us (0.47)
  waiting for transfers between devices: 207 us -> 0 us
  Pallas kernels: 0 us -> 131 us
  starting transfers between devices: 38.5 us -> 0 us
  matrix products: 15.8 us -> 0 us
  between operations: 13.6 us -> 0.01 us
  other arithmetic: 5.68 us -> 0 us
    reduce_scatter x1 -> x0, waiting for transfers between devices: 182 us -> none  [per_device(): total = lax.psum_scatter(terms, 'dp', scatter_dimension=1, tiled=True)]
    pallas_call x0 -> x1, Pallas kernels: none -> 131 us  [per_device(): pl.pallas_call(kernel, out_shape=jax.ShapeDtypeStruct((2, block, lat), BF...]
    ppermute x5 -> x0, starting transfers between devices: 38.5 us -> none  [the longest x1 22.3 us: per_device(): up_y1 = lax.ppermute(up_z, 'pipe', behind)]
    ppermute x5 -> x0, waiting for transfers between devices: 24.6 us -> none  [the longest x1 10.2 us: per_device(): up_y0 = lax.ppermute(grad_start[1, 0], 'pipe', mirror)]
    dot_general x12 -> x0, matrix products: 15.8 us -> none  [the longest x4 5.57 us: micro(): latent = jnp.dot(normed, pair[0], preferred_element_type=jnp.float32)]
    another operation x1 -> x0, other arithmetic: 3.6 us -> none  [per_device(): terms = jnp.stack([contract(n, q), contract(y, k)]).astype(jnp.bfloat16)]
  transfers between devices with their start and end apart: 6 -> 0, of which waited for: 4 -> 0; matrix products, arithmetic and copies ran while one was open for 5% -> 0% of each run, Pallas kernels for 0% -> 0%
where the time goes in v3:
time: 133 us
  Pallas kernels  131 us (98%)
  local copies, waits for them, and re-layouts  1.82 us (1%)
    pallas_call x1, Pallas kernels, per_device(): pl.pallas_call(kernel, out_shape=jax.ShapeDtypeStruct((2, block, lat), BF...  131 us

profile of v3, /device:TPU:24, one launch (start us, length us, event | category | flops | bytes accessed | tf_op | source)
XLA Modules:
  0.0 133.3 jit_solution(3509823138293546174)
XLA Ops:
  0.0 131.5 %relay_step.1 = bf16[2,448,256]{2,1,0:T(8,128)(2,1)} custom-call(bf16[1,2,7168,256]{3,2,1,0:T(8,128)(2,1)} %w_hbm.1, bf16[1,2,32,7168]{3,2,1,0:T(8,128)(2,1)} %sd_hbm.1, bf16[1,2,32,7168]{3,2,1,0:T(8,128)(2,1)} %su_hbm.1, bf16[2,1,32,7168]{3,2,1,0:T(8,128)(2,1)} %gs_hbm.1, bf16[1,7168]{1,0:T(2,128)(2,1)} %gm_ref.1, bf16[1,256]{1,0:T(2,128)(2,1)} %gl_ref.1), custom_call_target="tpu_custom_call" | custom-call | tf_op jit(solution)/shard_map/relay_step/pallas_call | solution.py:386
  131.5 1.8 %copy.8 = bf16[1,2,448,256]{3,2,1,0:T(8,128)(2,1)} copy(bf16[1,2,448,256]{3,2,1,0:T(8,128)(2,1)} %bitcast.1) | data formatting | bytes 917504

commit v4 on v3

--- a/solution.py
+++ b/solution.py
@@ -16,8 +16,8 @@
 
 
 def kernel(w_hbm, sd_hbm, su_hbm, gs_hbm, gm_ref, gl_ref, out_ref,
-           raw, w, xs, xg, ys, zr, inv, pf, pb, pr, kk, qq, acc, sb, rb, via,
-           lsem, in_s, in_r, a_s, a_r, rs_s, rs_r, ag_s, ag_r, rl_s, rl_r, gr_s, gr_r, via_s, via_r):
+           raw, w, xs, xg, ys, zr, inv, pf, pb, pr, kk, qq, acc, sb, rb, via, fw,
+           lsem, in_s, in_r, a_s, a_r, rs_s, rs_r, ag_s, ag_r, rl_s, rl_r, gr_s, gr_r, via_s, via_r, fs_s, fs_r, ff_s, ff_r):
     pipe = lax.axis_index("pipe")
     dp = lax.axis_index("dp")
     ranks = lax.axis_size("pipe")
@@ -53,6 +53,23 @@
     for d in greet:
         pl.semaphore_signal(barrier, inc=1, device_id=d, device_id_type=MESH)
 
+    edge = ranks // 2
+    is_edge = pipe == edge
+    is_end = pipe == edge - 1
+    stops = [{"pipe": edge + 2 * j, "dp": dp} for j in range(1, X)]
+    is_stop = jnp.logical_or(pipe == edge + 2, jnp.logical_or(pipe == edge + 4, pipe == edge + 6))
+    ends = {"pipe": edge - 1, "dp": dp}
+
+    @pl.when(jnp.logical_or(is_edge, is_end))
+    def _():
+        for d in stops:
+            pl.semaphore_signal(barrier, inc=1, device_id=d, device_id_type=MESH)
+
+    @pl.when(is_stop)
+    def _():
+        for d in ({"pipe": edge, "dp": dp}, ends):
+            pl.semaphore_signal(barrier, inc=1, device_id=d, device_id_type=MESH)
+
     def remote(src, dst, ss, rs, dev):
         return pltpu.make_async_remote_copy(
             src_ref=src, dst_ref=dst, send_sem=ss, recv_sem=rs, device_id=dev, device_id_type=MESH)
@@ -89,7 +106,20 @@
         sent.extend(cs)
         return cs
 
-    pl.semaphore_wait(barrier, len(greet))
+    turn = jnp.logical_or(is_edge, is_end)
+
+    @pl.when(turn)
+    def _():
+        pl.semaphore_wait(barrier, len(greet) + len(stops))
+
+    @pl.when(is_stop)
+    def _():
+        pl.semaphore_wait(barrier, len(greet) + 2)
+
+    @pl.when(jnp.logical_not(jnp.logical_or(turn, is_stop)))
+    def _():
+        pl.semaphore_wait(barrier, len(greet))
+
     up_x0 = send_up(UX0, xs.at[1])
     up_y0 = send_up(UY0, ys.at[1])
     down_x0 = send_down(DX0, xs.at[0])
@@ -186,6 +216,60 @@
     def relay(m):
         return remote(zr.at[m], ys.at[m + 2], rl_s.at[m], rl_r.at[m], before)
 
+    def relay_parts(m):
+        first = pl.ds(0, rows)
+        cs = [remote(zr.at[m, first, :], ys.at[m + 2, first, :], rl_s.at[m], rl_r.at[m], before)]
+        for j in range(1, X):
+            cs.append(remote(zr.at[m, pl.ds(j * rows, rows), :], fw.at[m], fs_s.at[m, j - 1], fs_r.at[m], stops[j - 1]))
+        return cs
+
+    def relay_on(m):
+        j = (pipe - edge) // 2
+        there = pl.ds(pl.multiple_of(j * rows, rows), rows)
+        return remote(fw.at[m], ys.at[m + 2, there, :], ff_s.at[m], ff_r.at[m, j - 1], ends)
+
+    def relay_start(m):
+        @pl.when(jnp.logical_and(pipe > 0, jnp.logical_not(is_edge)))
+        def _():
+            relay(m).start()
+
+        @pl.when(is_edge)
+        def _():
+            for c in relay_parts(m):
+                c.start()
+
+    def relay_pass(m):
+        @pl.when(is_stop)
+        def _():
+            remote(zr.at[m, pl.ds(0, rows), :], fw.at[m], fs_s.at[m, 0], fs_r.at[m], stops[0]).wait_recv()
+            relay_on(m).start()
+
+    def relay_end(m):
+        @pl.when(jnp.logical_and(pipe < ranks - 1, jnp.logical_not(is_end)))
+        def _():
+            relay(m).wait_recv()
+
+        @pl.when(is_end)
+        def _():
+            first = pl.ds(0, rows)
+            remote(zr.at[m, first, :], ys.at[m + 2, first, :], rl_s.at[m], rl_r.at[m], before).wait_recv()
+            for j in range(1, X):
+                remote(fw.at[m], ys.at[m + 2, pl.ds(j * rows, rows), :], ff_s.at[m], ff_r.at[m, j - 1], ends).wait_recv()
+
+    def relay_sent(m):
+        @pl.when(jnp.logical_and(pipe > 0, jnp.logical_not(is_edge)))
+        def _():
+            relay(m).wait_send()
+
+        @pl.when(is_edge)
+        def _():
+            for c in relay_parts(m):
+                c.wait_send()
+
+        @pl.when(is_stop)
+        def _():
+            relay_on(m).wait_send()
+
     def grads(half, m):
         def body(i, carry):
             cols = pl.ds(pl.multiple_of(i * STEP, STEP), STEP)
@@ -286,17 +370,14 @@
     gq0 = latent_q(0, s0, re0)
     arrive(gq0)
     input_grad(0)
-    down = relay(0)
-
-    @pl.when(pipe > 0)
-    def _():
-        down.start()
+    relay_start(0)
 
     inv[5] = inverse(UX1)
     inv[2] = inverse(DX1)
     arrive(gk0)
     grads(0, 0)
     grads(1, 0)
+    relay_pass(0)
     own_loads[DX1].wait()
     arrive(down_x1)
     rc2 = part_c(2)
@@ -316,15 +397,9 @@
     gq1 = latent_q(1, s1, re1)
     arrive(gq1)
     input_grad(1)
-    up = relay(1)
-
-    @pl.when(pipe > 0)
-    def _():
-        up.start()
-
-    @pl.when(pipe < ranks - 1)
-    def _():
-        down.wait_recv()
+    relay_start(1)
+
+    relay_end(0)
 
     @pl.when(pipe == ranks - 1)
     def _():
@@ -332,25 +407,22 @@
         ys[3] = jnp.zeros((tokens, quarter), BF)
 
     re2 = part_e(2)
+    relay_pass(1)
     arrive(gk1)
     grads(0, 1)
     grads(1, 1)
     gq2 = latent_q(2, s2, re2)
+
+    arrive(up_x1)
+    rc3 = part_c(3)
+    relay_end(1)
+    re3 = part_e(3)
+    up_a1.wait_recv()
+    s3, gk3 = latent_k(3, rc3)
     arrive(gk2)
     grads(1, 2)
     arrive(gq2)
     grads(0, 2)
-
-    arrive(up_x1)
-    rc3 = part_c(3)
-
-    @pl.when(pipe < ranks - 1)
-    def _():
-        up.wait_recv()
-
-    re3 = part_e(3)
-    up_a1.wait_recv()
-    s3, gk3 = latent_k(3, rc3)
     gq3 = latent_q(3, s3, re3)
     arrive(gk3)
     grads(1, 3)
@@ -368,10 +440,8 @@
     for c in sent + up_x1 + [up_a0, up_a1]:
         c.wait_send()
 
-    @pl.when(pipe > 0)
-    def _():
-        down.wait_send()
-        up.wait_send()
+    relay_sent(0)
+    relay_sent(1)
 
 
 def per_device(weights, gain_model, gain_latent, saved_down, saved_up, grad_start):
@@ -405,6 +475,7 @@
             pltpu.VMEM((2, 3, block, lat), BF),
             pltpu.VMEM((2, 3, block, lat), BF),
             pltpu.VMEM((2, block, lat), BF),
+            pltpu.VMEM((2, rows, quarter), BF),
             dma((9,)),
             dma((6, 4)), dma((6, 4)),
             dma((2,)), dma((2,)),
@@ -413,6 +484,7 @@
             dma((2,)), dma((2,)),
             dma((2, 3)), dma((2, 3)),
             dma((2,)), dma((2,)),
+            dma((2, 3)), dma((2,)), dma((2,)), dma((2, 3)),
         ],
         compiler_params=pltpu.CompilerParams(
             collective_id=0, has_side_effects=True, vmem_limit_bytes=56 << 20),

time: 133 us -> 127 us (0.955)
  Pallas kernels: 131 us -> 124 us
    pallas_call x1, Pallas kernels: 131 us -> 124 us  [per_device(): pl.pallas_call(kernel, out_shape=jax.ShapeDtypeStruct((2, block, lat), BF...]
where the time goes in v4:
time: 127 us; the launch traced here: 126 us
  Pallas kernels  124 us (98%)
  local copies, waits for them, and re-layouts  1.82 us (1%)
    pallas_call x1, Pallas kernels, per_device(): pl.pallas_call(kernel, out_shape=jax.ShapeDtypeStruct((2, block, lat), BF...  124 us

profile of v4, /device:TPU:24, one launch (start us, length us, event | category | flops | bytes accessed | tf_op | source)
XLA Modules:
  0.0 126.1 jit_solution(4605245620232017772)
XLA Ops:
  0.0 124.3 %relay_step.1 = bf16[2,448,256]{2,1,0:T(8,128)(2,1)} custom-call(bf16[1,2,7168,256]{3,2,1,0:T(8,128)(2,1)} %w_hbm.1, bf16[1,2,32,7168]{3,2,1,0:T(8,128)(2,1)} %sd_hbm.1, bf16[1,2,32,7168]{3,2,1,0:T(8,128)(2,1)} %su_hbm.1, bf16[2,1,32,7168]{3,2,1,0:T(8,128)(2,1)} %gs_hbm.1, bf16[1,7168]{1,0:T(2,128)(2,1)} %gm_ref.1, bf16[1,256]{1,0:T(2,128)(2,1)} %gl_ref.1), custom_call_target="tpu_custom_call" | custom-call | tf_op jit(solution)/shard_map/relay_step/pallas_call | solution.py:456
  124.3 1.8 %copy.8 = bf16[1,2,448,256]{3,2,1,0:T(8,128)(2,1)} copy(bf16[1,2,448,256]{3,2,1,0:T(8,128)(2,1)} %bitcast.1) | data formatting | bytes 917504

commit v5 on v4

--- a/solution.py
+++ b/solution.py
@@ -121,7 +121,6 @@
         pl.semaphore_wait(barrier, len(greet))
 
     up_x0 = send_up(UX0, xs.at[1])
-    up_y0 = send_up(UY0, ys.at[1])
     down_x0 = send_down(DX0, xs.at[0])
     down_y0 = send_down(DY0, ys.at[0])
     down_x1 = send_down(DX1, xs.at[2])
@@ -272,7 +271,7 @@
 
     def grads(half, m):
         def body(i, carry):
-            cols = pl.ds(pl.multiple_of(i * STEP, STEP), STEP)
+            cols = pl.ds(pl.multiple_of(i * 896, 896), 896)
             left = xg[m, :, cols] if half == 0 else ys[m, :, cols]
             right = qq[m, :, 0:lat] if half == 0 else kk[m]
             t = lax.dot_general(left, right, (((0,), (0,)), ((), ())), preferred_element_type=F32)
@@ -281,7 +280,7 @@
             else:
                 acc[half, cols, :] += t
             return carry
-        lax.fori_loop(0, quarter // STEP, body, 0)
+        lax.fori_loop(0, quarter // 896, body, 0)
 
     def far_block(k):
         return pl.ds(pl.multiple_of(lax.rem(z + k, Z) * block, 16), block)
@@ -366,6 +365,7 @@
     rc0 = part_c(0)
     arrive(down_y0)
     re0 = part_e(0)
+    up_y0 = send_up(UY0, ys.at[1])
     s0, gk0 = latent_k(0, rc0)
     gq0 = latent_q(0, s0, re0)
     arrive(gq0)
@@ -383,17 +383,17 @@
     rc2 = part_c(2)
     s2, gk2 = latent_k(2, rc2)
 
+    arrive(up_x0)
+    rc1 = part_c(1)
+    up_a0.wait_recv()
+    s1, gk1 = latent_k(1, rc1)
     for c in up_x0 + up_y0:
         c.wait_send()
     up_x1 = send_up(UX1, xs.at[3])
     up_a1 = remote(inv.at[5], inv.at[3], a_s.at[1], a_r.at[1], mirror[0])
     up_a1.start()
-    arrive(up_x0)
-    rc1 = part_c(1)
     arrive(up_y0)
     re1 = part_e(1)
-    up_a0.wait_recv()
-    s1, gk1 = latent_k(1, rc1)
     gq1 = latent_q(1, s1, re1)
     arrive(gq1)
     input_grad(1)

time: 127 us -> 124 us (0.976)
  Pallas kernels: 124 us -> 122 us
    pallas_call x1, Pallas kernels: 124 us -> 122 us  [per_device(): pl.pallas_call(kernel, out_shape=jax.ShapeDtypeStruct((2, block, lat), BF...]
where the time goes in v5:
time: 124 us
  Pallas kernels  122 us (98%)
  local copies, waits for them, and re-layouts  1.82 us (1%)
    pallas_call x1, Pallas kernels, per_device(): pl.pallas_call(kernel, out_shape=jax.ShapeDtypeStruct((2, block, lat), BF...  122 us

profile of v5, /device:TPU:24, one launch (start us, length us, event | category | flops | bytes accessed | tf_op | source)
XLA Modules:
  0.0 123.8 jit_solution(406861249646205750)
XLA Ops:
  0.0 122.0 %relay_step.1 = bf16[2,448,256]{2,1,0:T(8,128)(2,1)} custom-call(bf16[1,2,7168,256]{3,2,1,0:T(8,128)(2,1)} %w_hbm.1, bf16[1,2,32,7168]{3,2,1,0:T(8,128)(2,1)} %sd_hbm.1, bf16[1,2,32,7168]{3,2,1,0:T(8,128)(2,1)} %su_hbm.1, bf16[2,1,32,7168]{3,2,1,0:T(8,128)(2,1)} %gs_hbm.1, bf16[1,7168]{1,0:T(2,128)(2,1)} %gm_ref.1, bf16[1,256]{1,0:T(2,128)(2,1)} %gl_ref.1), custom_call_target="tpu_custom_call" | custom-call | tf_op jit(solution)/shard_map/relay_step/pallas_call | solution.py:456
  122.0 1.8 %copy.8 = bf16[1,2,448,256]{3,2,1,0:T(8,128)(2,1)} copy(bf16[1,2,448,256]{3,2,1,0:T(8,128)(2,1)} %bitcast.1) | data formatting | bytes 917504

commit v6 on v5

--- a/solution.py
+++ b/solution.py
@@ -39,10 +39,6 @@
     for j, (i, dst) in enumerate(((DX0, xs.at[0]), (DY0, ys.at[0]), (DX1, xs.at[2]))):
         own_loads[i] = pltpu.make_async_copy(inputs[i].at[:, mine], dst.at[here], lsem.at[4 + j])
     w_loads = [pltpu.make_async_copy(w_hbm.at[0, half, mine, :], w.at[half], lsem.at[7 + half]) for half in range(2)]
-    for c in [raw_loads[UX0][1], own_loads[DX0], w_loads[0], own_loads[DY0], w_loads[1],
-              raw_loads[DX0][1], raw_loads[UX1][1], raw_loads[DX1][1], own_loads[DX1]]:
-        c.start()
-
     mirror = [{"pipe": ranks - 1 - pipe, "dp": lax.rem(x + k, X) * Z + lax.rem(z + 2, Z)} for k in range(X)]
     xpeer = [{"pipe": pipe, "dp": lax.rem(x + k, X) * Z + z} for k in range(1, X)]
     zpeer = [{"pipe": pipe, "dp": x * Z + lax.rem(z + k, Z)} for k in range(1, Z)]
@@ -69,6 +65,10 @@
     def _():
         for d in ({"pipe": edge, "dp": dp}, ends):
             pl.semaphore_signal(barrier, inc=1, device_id=d, device_id_type=MESH)
+
+    for c in [raw_loads[UX0][1], own_loads[DX0], w_loads[0], own_loads[DY0], w_loads[1],
+              raw_loads[DX0][1], raw_loads[UX1][1], raw_loads[DX1][1], own_loads[DX1]]:
+        c.start()
 
     def remote(src, dst, ss, rs, dev):
         return pltpu.make_async_remote_copy(
@@ -406,8 +406,8 @@
         ys[2] = jnp.zeros((tokens, quarter), BF)
         ys[3] = jnp.zeros((tokens, quarter), BF)
 
+    relay_pass(1)
     re2 = part_e(2)
-    relay_pass(1)
     arrive(gk1)
     grads(0, 1)
     grads(1, 1)

time: 124 us -> 124 us (level)
  no operation moved by 1% of the time
where the time goes in v6:
time: 124 us
  Pallas kernels  122 us (98%)
  local copies, waits for them, and re-layouts  1.82 us (1%)
    pallas_call x1, Pallas kernels, per_device(): pl.pallas_call(kernel, out_shape=jax.ShapeDtypeStruct((2, block, lat), BF...  122 us

profile of v6, /device:TPU:24, one launch (start us, length us, event | category | flops | bytes accessed | tf_op | source)
XLA Modules:
  0.0 123.8 jit_solution(3559254559641664660)
XLA Ops:
  0.0 122.0 %relay_step.1 = bf16[2,448,256]{2,1,0:T(8,128)(2,1)} custom-call(bf16[1,2,7168,256]{3,2,1,0:T(8,128)(2,1)} %w_hbm.1, bf16[1,2,32,7168]{3,2,1,0:T(8,128)(2,1)} %sd_hbm.1, bf16[1,2,32,7168]{3,2,1,0:T(8,128)(2,1)} %su_hbm.1, bf16[2,1,32,7168]{3,2,1,0:T(8,128)(2,1)} %gs_hbm.1, bf16[1,7168]{1,0:T(2,128)(2,1)} %gm_ref.1, bf16[1,256]{1,0:T(2,128)(2,1)} %gl_ref.1), custom_call_target="tpu_custom_call" | custom-call | tf_op jit(solution)/shard_map/relay_step/pallas_call | solution.py:456
  122.0 1.8 %copy.8 = bf16[1,2,448,256]{3,2,1,0:T(8,128)(2,1)} copy(bf16[1,2,448,256]{3,2,1,0:T(8,128)(2,1)} %bitcast.1) | data formatting | bytes 917504
